TPU v7x, 128 devices: a whole 4x4x4 slice. The times are simulated.
128 devices in a mesh: atom: 16 (over x_hi, y, core), mode: 8 (over x_lo, z).
Axes of the slice: x: 4 (x_hi: 2, x_lo: 2; x = x_hi * 2 + x_lo), y: 4, z: 4, core: 2. Of those that a mesh axis runs over, the one named last changes fastest.
Arguments:
- features: float32 [128, 16384], P(None, 'atom'), may hold values from -6 to 6
- positions: float32 [3, 16384], P(None, 'atom'), may hold values from 0 to 1, as said below
- wavevectors: int32 [3, 8192], P(None, 'mode'), may hold values from -768 to 768, as said below
- mode_filter: float32 [128, 8192], P(None, 'mode'), may hold values from -12 to 12
- radial_mix: float32 [4, 128, 128], replicated, may hold values from -0.03125 to 0.03125
- radial_rates: float32 [4], replicated, may hold values from 0.2 to 3
- neighbour_ids: int32 [128, 5], P(('atom', 'mode')), may hold values from 0 to 127, as said below
- live_counts: int32 [128], P(('atom', 'mode')), may hold values from 1 to 5, as said below
- cotangent: float32 [128, 16384], P(None, ('atom', 'mode')), may hold values from -6 to 6
Outputs:
- layer_out: float32 [128, 16384], P(None, ('atom', 'mode'))
- grad_features: float32 [128, 16384], P(None, ('atom', 'mode'))
- grad_filter: float32 [128, 8192], P(None, 'mode')
Inputs may be any that keep to these rules, and one draw needn't show every extreme that they name: `positions`: row 0 of atom i lies between b / 128 and (b + 1) / 128, with b = i // 128; rows 1 and 2 lie anywhere in the range. `wavevectors`: row 0 lies between -768 and 768; rows 1 and 2 lie between -12 and 12. `neighbour_ids`: row b lists the 5 blocks (b + o) mod 128, o from -2 to 2, each once, in some order; only the first live_counts[b] slots are live. `live_counts`: some block has all 5 slots live.
All inputs are finite; a program needn't handle non-finite values.
Results may differ from a plain program's by a relative error of at most 0.00035.
Values sent between devices are 32-bit elements; how exact they have to be, the bound alone decides.
No kernel may reach another device: no remote copies, remote signals or barrier semaphores. Data moves between devices by JAX's collectives and lax.ppermute only.
A program may use at most 64 MiB of HBM per device.

v0:
```python
import jax
import jax.numpy as jnp
from jax import lax
from jax.experimental import pallas as pl
from jax.experimental.pallas import tpu as pltpu
from jax.sharding import PartitionSpec as P

BLOCK = 128
REACH = 2
SLOTS = 5
C = 128
ATOMS = 1024
MODES = 1024
HALF = 512
SHARE = 64
RADIAL = 4
ATOM_DEV = 16
MODE_DEV = 8
HALO_ROWS = 272

F32 = jnp.float32
BF16 = jnp.bfloat16
MAGIC = 12582912.0
VMEM = pltpu.VMEM

NT = (((1,), (1,)), ((), ()))
NN = (((1,), (0,)), ((), ()))


def dot(a, b, dims):
    return lax.dot_general(a, b, dims, preferred_element_type=F32)


def pieces(x):
    high = x.astype(BF16)
    low = (x - high.astype(F32)).astype(BF16)
    return high, low


def cos_sin_turns(t):
    r = t - ((t + MAGIC) - MAGIC)
    y = r * r
    s = r * (4.44287957 + y * (-7.30781668 + y * (3.59777418 + y * -0.79119939)))
    c = 1.4142135 + y * (
        -6.97885095 + y * (5.73946038 + y * (-1.88355791 + y * 0.31068803))
    )
    return 1.0 - s * s, s * c


ROWS = 32
TILE = 256


def tables_tile(pos_ref, wave_ref, tab_ref, first, tile):
    shard = lax.axis_index("atom")
    mid = (2 * shard + 1).astype(F32) * (1.0 / 32.0)
    for chunk in range(TILE // ROWS):
        at = tile * TILE + chunk * ROWS
        w = wave_ref[pl.ds(pl.multiple_of(first + at, ROWS), ROWS), :]
        start = ((w[:, 0:1] * (2 * shard + 1)) & 31).astype(F32) * (1.0 / 32.0)
        wf = w.astype(F32)
        w0 = jnp.broadcast_to(wf[:, 0:1], (ROWS, BLOCK))
        w1 = jnp.broadcast_to(wf[:, 1:2], (ROWS, BLOCK))
        w2 = jnp.broadcast_to(wf[:, 2:3], (ROWS, BLOCK))
        c0 = jnp.broadcast_to(start, (ROWS, BLOCK))
        for k in range(ATOMS // BLOCK):
            lanes = pl.ds(k * BLOCK, BLOCK)
            p0 = pos_ref[0:1, lanes] - mid
            p1 = pos_ref[1:2, lanes]
            p2 = pos_ref[2:3, lanes]
            t = w0 * p0 + (w1 * p1 + (w2 * p2 + c0))
            cos, sin = cos_sin_turns(t)
            ch, cl = pieces(cos)
            sh, sl = pieces(sin)
            tab_ref[at : at + ROWS, lanes] = ch
            tab_ref[HALF + at : HALF + at + ROWS, lanes] = sh
            tab_ref[2 * HALF + at : 2 * HALF + at + ROWS, lanes] = cl
            tab_ref[3 * HALF + at : 3 * HALF + at + ROWS, lanes] = sl


def sums_tile(tab_ref, rhs_ref, out_ref, tile):
    for trig in range(2):
        at = trig * HALF + tile * TILE
        both = dot(tab_ref[at : at + TILE, :], rhs_ref[...], NT)
        at = at + 2 * HALF
        rest = dot(tab_ref[at : at + TILE, :], rhs_ref[0:C, :], NT)
        out_ref[tile * TILE : (tile + 1) * TILE, trig * C : (trig + 1) * C] = (
            both[:, :C] + both[:, C:] + rest
        )


def tables_kernel(own, feat_ref, pos_ref, wave_ref, out_ref, tab_ref, rhs_ref):
    core = lax.axis_index("atom") % 2
    first = HALF * (core if own else 1 - core)
    high, low = pieces(feat_ref[...])
    rhs_ref[0:C, :] = high
    rhs_ref[C:, :] = low
    for tile in range(HALF // TILE):
        tables_tile(pos_ref, wave_ref, tab_ref, first, tile)
        sums_tile(tab_ref, rhs_ref, out_ref, tile)


def spec():
    return pl.BlockSpec(memory_space=VMEM)


def tables_call(own, feat, pos, wave):
    def body(*refs):
        tables_kernel(own, *refs)

    return pl.pallas_call(
        body,
        out_shape=(
            jax.ShapeDtypeStruct((HALF, 2 * C), F32),
            jax.ShapeDtypeStruct((4 * HALF, ATOMS), BF16),
        ),
        in_specs=[spec()] * 3,
        out_specs=(spec(), spec()),
        scratch_shapes=[VMEM((2 * C, ATOMS), BF16)],
        cost_estimate=pl.CostEstimate(
            flops=3 * 10**9, bytes_accessed=5 * 10**6, transcendentals=0
        ),
        name="tables_own" if own else "tables_other",
    )(feat, pos, wave)


def cot_kernel(cot_ref, tab_ref, out_ref, rhs_ref):
    for k in range(MODE_DEV):
        high, low = pieces(cot_ref[k, 0:C, :])
        rhs_ref[0:C, k * BLOCK : (k + 1) * BLOCK] = high
        rhs_ref[C:, k * BLOCK : (k + 1) * BLOCK] = low
    for tile in range(HALF // TILE):
        sums_tile(tab_ref, rhs_ref, out_ref, tile)


def cot_call(cot, tab):
    return pl.pallas_call(
        cot_kernel,
        out_shape=jax.ShapeDtypeStruct((HALF, 2 * C), F32),
        in_specs=[spec()] * 2,
        out_specs=spec(),
        scratch_shapes=[VMEM((2 * C, ATOMS), BF16)],
        cost_estimate=pl.CostEstimate(
            flops=2 * 10**9, bytes_accessed=5 * 10**6, transcendentals=0
        ),
        name="cot_sums",
    )(cot, tab)


def turned(sums_ref, trig):
    return jnp.concatenate(
        [
            sums_ref[k * C : (k + 1) * C, trig * C : (trig + 1) * C].T
            for k in range(HALF // C)
        ],
        axis=1,
    )


def give_back_kernel(
    with_grad, own_ref, oth_ref, filt_ref, tab_own_ref, tab_oth_ref, *rest
):
    if with_grad:
        fown_ref, foth_ref, out_ref, grad_ref, lhs_ref = rest
    else:
        out_ref, lhs_ref = rest
    core = lax.axis_index("atom") % 2
    scale = 1.0 / (ATOM_DEV * ATOMS)
    for half in range(2):
        ref = (own_ref, oth_ref)[half]
        at = pl.multiple_of(HALF * (core if half == 0 else 1 - core), HALF)
        filt = filt_ref[:, pl.ds(at, HALF)] * scale
        grad = None
        for trig in range(2):
            sums = turned(ref, trig)
            if with_grad:
                term = turned((fown_ref, foth_ref)[half], trig) * sums
                grad = term if grad is None else grad + term
            high, low = pieces(filt * sums)
            lanes = pl.ds((2 * half + trig) * HALF, HALF)
            lhs_ref[0:C, lanes] = high
            lhs_ref[C:, lanes] = low
        if with_grad:
            grad_ref[:, pl.ds(at, HALF)] = grad * scale
    width = 2 * BLOCK
    for k in range(ATOMS // width):
        lanes = slice(k * width, (k + 1) * width)
        total = None
        for half in range(2):
            tab = (tab_own_ref, tab_oth_ref)[half]
            at = slice(2 * half * HALF, 2 * (half + 1) * HALF)
            both = dot(lhs_ref[:, at], tab[0 : 2 * HALF, lanes], NN)
            more = dot(lhs_ref[0:C, at], tab[2 * HALF :, lanes], NN)
            part = both[:C] + both[C:] + more
            total = part if total is None else total + part
        out_ref[2 * k] = total[:, :BLOCK]
        out_ref[2 * k + 1] = total[:, BLOCK:]


def give_back_call(own, oth, filt, tab_own, tab_oth, fsums=None):
    with_grad = fsums is not None

    def body(*refs):
        give_back_kernel(with_grad, *refs)

    out_shape = [jax.ShapeDtypeStruct((MODE_DEV, C, BLOCK), F32)]
    args = [own, oth, filt, tab_own, tab_oth]
    if with_grad:
        out_shape.append(jax.ShapeDtypeStruct((C, MODES), F32))
        args.extend(fsums)
    return pl.pallas_call(
        body,
        out_shape=tuple(out_shape),
        in_specs=[spec()] * len(args),
        out_specs=tuple(spec() for _ in out_shape),
        scratch_shapes=[VMEM((2 * C, 4 * HALF), BF16)],
        cost_estimate=pl.CostEstimate(
            flops=2 * 10**9, bytes_accessed=10**7, transcendentals=0
        ),
        name="give_back_cot" if with_grad else "give_back_feat",
    )(*args)


def near_kernel(
    left_ref,
    right_ref,
    feat_ref,
    pos_ref,
    cot_ref,
    mix_ref,
    rate_ref,
    live_ref,
    out_ref,
    back_ref,
    ext_ref,
    rhs_ref,
):
    own = lax.axis_index("mode")
    pad = REACH * BLOCK
    ext_ref[:, 0:pad] = left_ref[...]
    ext_ref[:, pad + ATOMS :] = right_ref[...]
    ext_ref[0:C, pad : pad + ATOMS] = feat_ref[...]
    ext_ref[C : C + 3, pad : pad + ATOMS] = pos_ref[...]
    for k in range(MODE_DEV):
        ext_ref[136:272, pad + k * BLOCK : pad + (k + 1) * BLOCK] = cot_ref[k]
    shard = lax.axis_index("atom")
    total_blocks = ATOM_DEV * MODE_DEV

    def unit(block, row):
        return row * float(total_blocks) - block.astype(F32)

    def halves(row):
        q = row - 0.5
        y = q * q
        s = q * (
            3.14159265
            + y
            * (-5.16771276 + y * (2.55016332 + y * (-0.5992522 + y * (0.0820504 - 0.00702839 * y))))
        )
        c = 1.0 + y * (
            -4.93480214
            + y * (4.05870916 + y * (-1.335212 + y * (0.23493731 - 0.02439632 * y)))
        )
        return -s, c

    me = shard * MODE_DEV + own
    here = ext_ref[C : C + 8, pl.ds(pl.multiple_of(pad + own * BLOCK, BLOCK), BLOCK)]
    u_own = unit(me, here[0:1])
    c1, s1 = halves(here[1:2])
    c2, s2 = halves(here[2:3])
    rows = jnp.concatenate([u_own, c1, s1, c2, s2, u_own, u_own, u_own], axis=0)
    columns = jnp.concatenate([rows] * (BLOCK // 8), axis=0).T
    wide = [jnp.broadcast_to(columns[:, k : k + 1], (BLOCK, BLOCK)) for k in range(5)]
    span = 2 * REACH + 1
    dist = []
    live = live_ref[0:1, :]
    for o in range(span):
        at = pl.ds(pl.multiple_of((own + o) * BLOCK, BLOCK), BLOCK)
        block = ext_ref[:, at]
        there = lax.rem(me + o - REACH + total_blocks, total_blocks)
        near = block[C : C + 8]
        x = wide[0] - (unit(there, near[0:1]) + float(o - REACH))
        d1c, d1s = halves(near[1:2])
        d2c, d2s = halves(near[2:3])
        y = x * x
        z = y * (3.14159265 / total_blocks) ** 2
        d = y * (1.0 + z * (-1.0 / 3.0 + z * (2.0 / 45.0)))
        e1 = wide[2] * d1c - wide[1] * d1s
        e2 = wide[4] * d2c - wide[3] * d2s
        d = d + (e1 * e1 + e2 * e2) * (2.0 / 3.14159265) ** 2
        dist.append(d)
        lanes = slice(o * BLOCK, (o + 1) * BLOCK)
        high, low = pieces(block[0:C] * live[0:1, o : o + 1])
        rhs_ref[0:C, lanes] = high
        rhs_ref[2 * C : 3 * C, lanes] = low
        lists_me = block[264:265, span - 1 - o : span - o]
        high, low = pieces(block[136 : 136 + C] * lists_me)
        rhs_ref[C : 2 * C, lanes] = high
        rhs_ref[3 * C :, lanes] = low
    out = ext_ref[0:C, pl.ds(pl.multiple_of(pad + own * BLOCK, BLOCK), BLOCK)]
    back = ext_ref[136 : 136 + C, pl.ds(pl.multiple_of(pad + own * BLOCK, BLOCK), BLOCK)]
    for r in range(RADIAL):
        rate = rate_ref[r]
        highs, lows = [], []
        for o in range(span):
            high, low = pieces(jnp.exp(dist[o] * -rate))
            highs.append(high)
            lows.append(low)
        weights_high = jnp.concatenate(highs, axis=1)
        weights_low = jnp.concatenate(lows, axis=1)
        both = dot(rhs_ref[...], weights_high, NT)
        got = (
            both[: 2 * C]
            + both[2 * C :]
            + dot(rhs_ref[0 : 2 * C, :], weights_low, NT)
        )
        high, low = pieces(got)
        mix = mix_ref[r]
        mh, ml = pieces(mix)
        th, tl = pieces(mix.T)
        out = out + (
            dot(th, high[:C], NN) + dot(th, low[:C], NN) + dot(tl, high[:C], NN)
        )
        back = back + (
            dot(mh, high[C:], NN) + dot(mh, low[C:], NN) + dot(ml, high[C:], NN)
        )
    out_ref[...] = out
    back_ref[...] = back


def near_call(left, right, feat, pos, cot, mix, rates, live):
    return pl.pallas_call(
        near_kernel,
        out_shape=(
            jax.ShapeDtypeStruct((C, BLOCK), F32),
            jax.ShapeDtypeStruct((C, BLOCK), F32),
        ),
        in_specs=[spec()] * 6 + [pl.BlockSpec(memory_space=pltpu.SMEM)] + [spec()],
        out_specs=(spec(), spec()),
        scratch_shapes=[
            VMEM((HALO_ROWS, ATOMS + 2 * REACH * BLOCK), F32),
            VMEM((4 * C, (2 * REACH + 1) * BLOCK), BF16),
        ],
        cost_estimate=pl.CostEstimate(
            flops=2 * 10**9, bytes_accessed=2 * 10**6, transcendentals=3 * 10**5
        ),
        name="near_blocks",
    )(left, right, feat, pos, cot, mix, rates, live)


def per_device(
    features,
    positions,
    wavevectors,
    mode_filter,
    radial_mix,
    radial_rates,
    neighbour_ids,
    live_counts,
    cotangent,
):
    core_swap = [(i, i ^ 1) for i in range(ATOM_DEV)]
    chips = [[c + 2 * i for i in range(ATOM_DEV // 2)] for c in range(2)]
    up = [(i, (i + 1) % ATOM_DEV) for i in range(ATOM_DEV)]
    down = [((i + 1) % ATOM_DEV, i) for i in range(ATOM_DEV)]

    def exchange(x):
        return lax.all_to_all(x, "atom", 0, 0, axis_index_groups=chips, tiled=True)

    me = lax.axis_index("atom") * MODE_DEV + lax.axis_index("mode")
    offset = jnp.mod(neighbour_ids[0] - me + REACH, ATOM_DEV * MODE_DEV)
    slots = jnp.arange(SLOTS, dtype=jnp.int32)
    hit = (offset[:, None] == jnp.arange(BLOCK, dtype=jnp.int32)[None, :]) & (
        slots[:, None] < live_counts[0]
    )
    live = jnp.broadcast_to(jnp.sum(hit.astype(F32), axis=0)[None, :], (8, BLOCK))
    packed = jnp.concatenate([cotangent, live], axis=0)
    cot = lax.all_to_all(
        jnp.broadcast_to(packed[None], (MODE_DEV, *packed.shape)), "mode", 0, 0, tiled=True
    )

    wave = wavevectors.T
    f_oth, tab_oth = tables_call(False, features, positions, wave)
    f_got = lax.ppermute(f_oth, "atom", core_swap)
    f_own, tab_own = tables_call(True, features, positions, wave)
    f_parts = exchange((f_own + f_got).reshape(8, SHARE, 2 * C))
    c_oth = cot_call(cot, tab_oth)
    c_got = lax.ppermute(c_oth, "atom", core_swap)
    c_own = cot_call(cot, tab_own)
    c_parts = exchange((c_own + c_got).reshape(8, SHARE, 2 * C))

    def halo(first):
        blocks = slice(first // BLOCK, first // BLOCK + REACH)
        ours = cot[blocks].transpose(1, 0, 2).reshape(C + 8, REACH * BLOCK)
        lanes = slice(first, first + REACH * BLOCK)
        return jnp.concatenate(
            [
                features[:, lanes],
                positions[:, lanes],
                jnp.zeros((5, REACH * BLOCK), F32),
                ours,
            ],
            axis=0,
        )

    left = lax.ppermute(halo(ATOMS - REACH * BLOCK), "atom", up)
    right = lax.ppermute(halo(0), "atom", down)
    near_out, near_back = near_call(
        left, right, features, positions, cot, radial_mix, radial_rates, live
    )

    def spread(parts):
        share = jnp.sum(parts, axis=0)
        own = exchange(jnp.broadcast_to(share[None], (8, *share.shape))).reshape(HALF, 2 * C)
        return own, lax.ppermute(own, "atom", core_swap)

    fs_own, fs_oth = spread(f_parts)
    (long_part,) = give_back_call(fs_own, fs_oth, mode_filter, tab_own, tab_oth)
    long_parts = lax.all_to_all(long_part, "mode", 0, 0, tiled=True)
    cs_own, cs_oth = spread(c_parts)
    back_part, grad_filter = give_back_call(
        cs_own, cs_oth, mode_filter, tab_own, tab_oth, (fs_own, fs_oth)
    )
    back_parts = lax.all_to_all(back_part, "mode", 0, 0, tiled=True)
    layer_out = near_out + jnp.sum(long_parts, axis=0)
    grad_features = near_back + jnp.sum(back_parts, axis=0)
    return (layer_out, grad_features, grad_filter)


def solution(mesh):
    in_specs = (
        P(None, "atom"),
        P(None, "atom"),
        P(None, "mode"),
        P(None, "mode"),
        P(),
        P(),
        P(("atom", "mode"), None),
        P(("atom", "mode")),
        P(None, ("atom", "mode")),
    )
    out_specs = (P(None, ("atom", "mode")), P(None, ("atom", "mode")), P(None, "mode"))
    return jax.shard_map(
        per_device, mesh=mesh, in_specs=in_specs, out_specs=out_specs, check_vma=False
    )
```

profile of v0, /device:TPU:0, one launch (start us, length us, event | category | flops | bytes accessed | tf_op | source)
XLA Modules:
  0.0 127.0 jit_solution(2670721570406847860)
XLA Ops:
  0.6 1.7 %copy.18 = s32[3,1024]{0,1:T(8,128)} copy(s32[3,1024]{1,0:T(4,128)} %param.11) | data formatting | bytes 24576 | tf_op args[2]
  2.4 0.0 copy-start.12
  2.4 6.4 %tables_other.1 = (f32[512,256]{1,0:T(8,128)}, bf16[2048,1024]{1,0:T(8,128)(2,1)}) custom-call(f32[128,1024]{1,0:T(8,128)} %refs_0_.3, f32[3,1024]{1,0:T(4,128)} %refs_1_.3, s32[1024,3]{1,0:T(8,128)} %bitcast.24), custom_call_target="tpu_custom_call" | custom-call | flops 3000000000 | bytes 5000000 | tf_op jit(solution)/shard_map/tables_other/pallas_call | solution.py:111
  8.8 0.0 collective-permute-start.2
  9.5 0.0 copy-done.12
  9.5 0.1 convert_reduce_fusion
  9.6 0.0 copy-done.7
  9.6 0.0 copy-start.8
  9.6 0.9 broadcast_in_dim.9
  10.5 6.4 %all-to-all-start = ((f32[8,136,128]{2,1,0:T(8,128)}), f32[8,136,128]{2,1,0:T(8,128)S(1)}, u32[]{:S(2)}, u32[]{:S(2)}) async-start(f32[8,136,128]{2,1,0:T(8,128)} %broadcast_in_dim.9), calls=%async_computation | async-start | bytes 1114112 | tf_op jit(solution)/shard_map/all_to_all | solution.py:378
  16.9 6.5 %tables_own.1 = (f32[512,256]{1,0:T(8,128)}, bf16[2048,1024]{1,0:T(8,128)(2,1)}) custom-call(f32[128,1024]{1,0:T(8,128)} %refs_0_.3, f32[3,1024]{1,0:T(4,128)} %refs_1_.3, s32[1024,3]{1,0:T(8,128)} %bitcast.25), custom_call_target="tpu_custom_call" | custom-call | flops 3000000000 | bytes 5000000 | tf_op jit(solution)/shard_map/tables_own/pallas_call | solution.py:111
  23.4 0.0 copy-done.8
  23.4 0.0 collective-permute-done.2
  23.4 1.9 %add.39 = f32[512,256]{1,0:T(8,128)} add(f32[512,256]{1,0:T(8,128)} %get-tuple-element.12, f32[512,256]{1,0:T(8,128)S(1)} %collective-permute-done.2) | non-fusion elementwise | flops 131072 | bytes 1572864 | tf_op jit(solution)/shard_map/add | solution.py:386
  25.3 2.0 %all-to-all-done.cot_ref = f32[8,136,128]{2,1,0:T(8,128)S(1)} async-done(((f32[8,136,128]{2,1,0:T(8,128)}), f32[8,136,128]{2,1,0:T(8,128)S(1)}, u32[]{:S(2)}, u32[]{:S(2)}) %all-to-all-start) | async-done | bytes 557088 | tf_op jit(solution)/shard_map/all_to_all | solution.py:378
  27.3 0.0 copy-start.3
  27.3 6.6 %all-to-all-start.1 = ((f32[8,64,256]{2,1,0:T(8,128)}), f32[8,64,256]{2,1,0:T(8,128)S(1)}, u32[]{:S(2)}, u32[]{:S(2)}) async-start(f32[8,64,256]{2,1,0:T(8,128)} %bitcast.5), calls=%async_computation.1 | async-start | bytes 1048576 | tf_op jit(solution)/shard_map/all_to_all | solution.py:368
  33.9 0.0 copy-done.3
  33.9 4.4 %cot_sums.3 = f32[512,256]{1,0:T(8,128)} custom-call(f32[8,136,128]{2,1,0:T(8,128)} %copy-done.3, bf16[2048,1024]{1,0:T(8,128)(2,1)} %get-tuple-element.15.refs_4_.tab_ref), custom_call_target="tpu_custom_call" | custom-call | flops 2000000000 | bytes 5000000 | tf_op jit(solution)/shard_map/cot_sums/pallas_call | solution.py:137
  38.4 0.0 collective-permute-start.4
  38.4 5.5 %all-to-all-done.1 = f32[8,64,256]{2,1,0:T(8,128)S(1)} async-done(((f32[8,64,256]{2,1,0:T(8,128)}), f32[8,64,256]{2,1,0:T(8,128)S(1)}, u32[]{:S(2)}, u32[]{:S(2)}) %all-to-all-start.1) | async-done | bytes 524320 | tf_op jit(solution)/shard_map/all_to_all | solution.py:368
  43.9 0.8 broadcast_in_dim.10
  44.8 3.5 %all-to-all-start.2 = ((f32[8,64,256]{2,1,0:T(8,128)}), f32[8,64,256]{2,1,0:T(8,128)S(1)}, u32[]{:S(2)}, u32[]{:S(2)}) async-start(f32[8,64,256]{2,1,0:T(8,128)} %broadcast_in_dim.10), calls=%async_computation.2 | async-start | bytes 1048576 | tf_op jit(solution)/shard_map/all_to_all | solution.py:368
  48.3 0.0 copy-start.6
  48.3 4.5 %cot_sums.2 = f32[512,256]{1,0:T(8,128)} custom-call(f32[8,136,128]{2,1,0:T(8,128)} %copy-done.3, bf16[2048,1024]{1,0:T(8,128)(2,1)} %get-tuple-element.14.refs_3_.tab_ref), custom_call_target="tpu_custom_call" | custom-call | flops 2000000000 | bytes 5000000 | tf_op jit(solution)/shard_map/cot_sums/pallas_call | solution.py:137
  52.8 0.0 collective-permute-done.4
  52.8 2.0 %add.41 = f32[512,256]{1,0:T(8,128)} add(f32[512,256]{1,0:T(8,128)} %cot_sums.2, f32[512,256]{1,0:T(8,128)S(1)} %collective-permute-done.4) | non-fusion elementwise | flops 131072 | bytes 1572864 | tf_op jit(solution)/shard_map/add | solution.py:390
  54.7 3.6 %all-to-all-done.2 = f32[8,64,256]{2,1,0:T(8,128)S(1)} async-done(((f32[8,64,256]{2,1,0:T(8,128)}), f32[8,64,256]{2,1,0:T(8,128)S(1)}, u32[]{:S(2)}, u32[]{:S(2)}) %all-to-all-start.2) | async-done | bytes 524320 | tf_op jit(solution)/shard_map/all_to_all | solution.py:368
  58.3 3.6 %all-to-all-start.4 = ((f32[8,64,256]{2,1,0:T(8,128)}), f32[8,64,256]{2,1,0:T(8,128)S(1)}, u32[]{:S(2)}, u32[]{:S(2)}) async-start(f32[8,64,256]{2,1,0:T(8,128)} %bitcast.7), calls=%async_computation.4 | async-start | bytes 1048576 | tf_op jit(solution)/shard_map/all_to_all | solution.py:368
  61.9 0.2 collective-permute-start.3
  62.1 0.0 copy-done.6
  62.2 0.1 pad.6.clone
  62.2 9.7 %all-to-all-done.4 = f32[8,64,256]{2,1,0:T(8,128)S(1)} async-done(((f32[8,64,256]{2,1,0:T(8,128)}), f32[8,64,256]{2,1,0:T(8,128)S(1)}, u32[]{:S(2)}, u32[]{:S(2)}) %all-to-all-start.4) | async-done | bytes 524320 | tf_op jit(solution)/shard_map/all_to_all | solution.py:368
  72.0 0.8 broadcast_in_dim.11
  72.8 3.5 %all-to-all-start.5 = ((f32[8,64,256]{2,1,0:T(8,128)}), f32[8,64,256]{2,1,0:T(8,128)S(1)}, u32[]{:S(2)}, u32[]{:S(2)}) async-start(f32[8,64,256]{2,1,0:T(8,128)} %broadcast_in_dim.11), calls=%async_computation.5 | async-start | bytes 1048576 | tf_op jit(solution)/shard_map/all_to_all | solution.py:368
  76.3 0.0 copy-done.9
  76.3 0.0 copy-done.4
  76.4 10.0 %all-to-all-done.5 = f32[8,64,256]{2,1,0:T(8,128)S(1)} async-done(((f32[8,64,256]{2,1,0:T(8,128)}), f32[8,64,256]{2,1,0:T(8,128)S(1)}, u32[]{:S(2)}, u32[]{:S(2)}) %all-to-all-start.5) | async-done | bytes 524320 | tf_op jit(solution)/shard_map/all_to_all | solution.py:368
  86.4 0.0 collective-permute-start.5
  86.4 0.0 collective-permute-done.3.refs_1_.refs_6_
  86.4 0.0 copy-done
  86.4 0.0 copy-start.1
  86.4 0.8 copy-done.1
  87.2 6.6 %give_back_feat.1 = f32[8,128,128]{2,1,0:T(8,128)} custom-call(f32[512,256]{1,0:T(8,128)} %bitcast.20, f32[512,256]{1,0:T(8,128)} %copy-done.1, f32[128,1024]{1,0:T(8,128)} %refs_2_.3, bf16[2048,1024]{1,0:T(8,128)(2,1)} %get-tuple-element.14.refs_3_.tab_ref, bf16[2048,1024]{1,0:T(8,128)(2,1)} %get-tuple-element.15.refs_4_.tab_ref), custom_call_target="tpu_custom_call" | custom-call | flops 2000000000 | bytes 10000000 | tf_op jit(solution)/shard_map/give_back_feat/pallas_call | solution.py:211
  93.8 7.0 %all-to-all-start.3 = ((f32[8,128,128]{2,1,0:T(8,128)}), f32[8,128,128]{2,1,0:T(8,128)S(1)}, u32[]{:S(2)}, u32[]{:S(2)}) async-start(f32[8,128,128]{2,1,0:T(8,128)} %give_back_feat.1), calls=%async_computation.3 | async-start | bytes 1048576 | tf_op jit(solution)/shard_map/all_to_all | solution.py:419
  100.8 0.1 pad_maximum_fusion.1
  100.9 2.6 %collective-permute-start.1 = (f32[272,256]{1,0:T(8,128)S(1)}, f32[272,256]{1,0:T(8,128)S(1)}, u32[]{:S(2)}, u32[]{:S(2)}) collective-permute-start(f32[272,256]{1,0:T(8,128)S(1)} %get-tuple-element.25), channel_id=1, source_target_pairs={{8,0},{16,8},{24,16},{32,24},{40,32},{48,40},{56,48},{64,56},{72,6... | collective-permute-start | bytes 835592 | tf_op jit(solution)/shard_map/ppermute | solution.py:407
  103.5 0.0 collective-permute-start
  103.5 0.0 collective-permute-done.5.refs_1_
  103.5 0.0 copy-done.2
  103.5 0.0 copy-start.5
  103.5 0.8 copy-done.5
  104.3 6.8 %give_back_cot.1 = (f32[8,128,128]{2,1,0:T(8,128)}, f32[128,1024]{1,0:T(8,128)}) custom-call(f32[512,256]{1,0:T(8,128)} %bitcast.23, f32[512,256]{1,0:T(8,128)} %copy-done.5, f32[128,1024]{1,0:T(8,128)} %refs_2_.3, bf16[2048,1024]{1,0:T(8,128)(2,1)} %get-tuple-element.14.refs_3_.tab_ref, bf16[2048,1024]{1,0:T(8,128)(2,1)} %get-tuple-element.15.refs_4_.tab_ref, ...), custom_call_target="tpu_custom_call" | custom-call | flops 2000000000 | bytes 10000000 | tf_op jit(solution)/shard_map/give_back_cot/pallas_call | solution.py:211
  111.1 0.0 all-to-all-done.3
  111.1 4.8 %all-to-all-start.6 = ((f32[8,128,128]{2,1,0:T(8,128)}), f32[8,128,128]{2,1,0:T(8,128)S(1)}, u32[]{:S(2)}, u32[]{:S(2)}) async-start(f32[8,128,128]{2,1,0:T(8,128)} %get-tuple-element.17), calls=%async_computation.6 | async-start | bytes 1048576 | tf_op jit(solution)/shard_map/all_to_all | solution.py:424
  115.9 0.0 collective-permute-done.1.right_ref
  115.9 0.0 copy-start.10
  115.9 0.0 collective-permute-done.left_ref
  115.9 0.7 copy-done.10
  116.6 0.7 copy-done.11
  117.3 4.6 %near_blocks.1 = (f32[128,128]{1,0:T(8,128)}, f32[128,128]{1,0:T(8,128)}) custom-call(f32[272,256]{1,0:T(8,128)} %copy-done.11, f32[272,256]{1,0:T(8,128)} %copy-done.10, f32[128,1024]{1,0:T(8,128)} %refs_0_.3, f32[3,1024]{1,0:T(4,128)} %refs_1_.3, f32[8,136,128]{2,1,0:T(8,128)} %copy-done.3, f32[4,128,128]{2,1,0:T(8,128)} %mix_ref.1, f32[4]{0:T(128)} %rate_ref.1, ...), custom_call_target="tpu_custom_call" | custom-call | flops 2000000000 | bytes 2000000 | tf_op jit(solution)/shard_map/near_blocks/pallas_call | solution.py:332
  122.0 1.5 %add.40 = f32[128,128]{1,0:T(8,128)} add(f32[128,128]{1,0:T(8,128)} %get-tuple-element.11, f32[128,128]{1,0:T(8,128)S(1)} %reduce_sum.47) | non-fusion elementwise | flops 16384 | bytes 196608 | tf_op jit(solution)/shard_map/add | solution.py:425
  123.5 2.0 %all-to-all-done.6 = f32[8,128,128]{2,1,0:T(8,128)S(1)} async-done(((f32[8,128,128]{2,1,0:T(8,128)}), f32[8,128,128]{2,1,0:T(8,128)S(1)}, u32[]{:S(2)}, u32[]{:S(2)}) %all-to-all-start.6) | async-done | bytes 524320 | tf_op jit(solution)/shard_map/all_to_all | solution.py:424
  125.6 1.5 %add.42 = f32[128,128]{1,0:T(8,128)} add(f32[128,128]{1,0:T(8,128)} %get-tuple-element.16, f32[128,128]{1,0:T(8,128)S(1)} %reduce_sum.49) | non-fusion elementwise | flops 16384 | bytes 196608 | tf_op jit(solution)/shard_map/add | solution.py:426
  (19 shorter events, 0.2 us)
Async XLA Ops:
  2.4 7.1 %copy-start.12 = (s32[1,5]{1,0:T(1,128)S(1)}, s32[1,5]{1,0:T(1,128)}, u32[]{:S(2)}) copy-start(s32[1,5]{1,0:T(1,128)} %param.15) | copy-start | bytes 64
  2.4 7.2 %copy-start.7 = (f32[128,128]{1,0:T(8,128)S(1)}, f32[128,128]{1,0:T(8,128)}, u32[]{:S(2)}) copy-start(f32[128,128]{1,0:T(8,128)} %param.17) | copy-start | bytes 196612
  8.8 14.6 %collective-permute-start.2 = (f32[512,256]{1,0:T(8,128)}, f32[512,256]{1,0:T(8,128)S(1)}, u32[]{:S(2)}, u32[]{:S(2)}) collective-permute-start(f32[512,256]{1,0:T(8,128)} %get-tuple-element.13), channel_id=1, source_target_pairs={{0,8},{8,0},{16,24},{24,16},{32,40},{40,32},{48,56},{56,48},{64,72... | collective-permute-start | bytes 1572872 | tf_op jit(solution)/shard_map/ppermute | solution.py:384
  9.6 13.8 %copy-start.8 = (f32[8,128]{1,0:T(8,128)}, f32[8,128]{1,0:T(8,128)S(1)}, u32[]{:S(2)}) copy-start(f32[8,128]{1,0:T(8,128)S(1)} %broadcast_in_dim.8.live_ref) | copy-start | bytes 12292
  10.5 16.8 %all-to-all-start = ((f32[8,136,128]{2,1,0:T(8,128)}), f32[8,136,128]{2,1,0:T(8,128)S(1)}, u32[]{:S(2)}, u32[]{:S(2)}) async-start(f32[8,136,128]{2,1,0:T(8,128)} %broadcast_in_dim.9), calls=%async_computation | async-start | bytes 1114112 | tf_op jit(solution)/shard_map/all_to_all | solution.py:378
  27.3 6.6 %copy-start.3 = (f32[8,136,128]{2,1,0:T(8,128)}, f32[8,136,128]{2,1,0:T(8,128)S(1)}, u32[]{:S(2)}) copy-start(f32[8,136,128]{2,1,0:T(8,128)S(1)} %all-to-all-done.cot_ref) | copy-start | bytes 1671172
  27.3 16.6 %all-to-all-start.1 = ((f32[8,64,256]{2,1,0:T(8,128)}), f32[8,64,256]{2,1,0:T(8,128)S(1)}, u32[]{:S(2)}, u32[]{:S(2)}) async-start(f32[8,64,256]{2,1,0:T(8,128)} %bitcast.5), calls=%async_computation.1 | async-start | bytes 1048576 | tf_op jit(solution)/shard_map/all_to_all | solution.py:368
  38.4 14.4 %collective-permute-start.4 = (f32[512,256]{1,0:T(8,128)}, f32[512,256]{1,0:T(8,128)S(1)}, u32[]{:S(2)}, u32[]{:S(2)}) collective-permute-start(f32[512,256]{1,0:T(8,128)} %cot_sums.3), channel_id=1, source_target_pairs={{0,8},{8,0},{16,24},{24,16},{32,40},{40,32},{48,56},{56,48},{64,72... | collective-permute-start | bytes 1572872 | tf_op jit(solution)/shard_map/ppermute | solution.py:388
  44.8 13.5 %all-to-all-start.2 = ((f32[8,64,256]{2,1,0:T(8,128)}), f32[8,64,256]{2,1,0:T(8,128)S(1)}, u32[]{:S(2)}, u32[]{:S(2)}) async-start(f32[8,64,256]{2,1,0:T(8,128)} %broadcast_in_dim.10), calls=%async_computation.2 | async-start | bytes 1048576 | tf_op jit(solution)/shard_map/all_to_all | solution.py:368
  48.3 13.8 %copy-start.6 = (f32[128,1024]{1,0:T(8,128)S(1)}, f32[128,1024]{1,0:T(8,128)}, u32[]{:S(2)}) copy-start(f32[128,1024]{1,0:T(8,128)} %refs_0_.3) | copy-start | bytes 1572868
  52.8 23.5 %copy-start.9 = (f32[3,1024]{1,0:T(4,128)S(1)}, f32[3,1024]{1,0:T(4,128)}, u32[]{:S(2)}) copy-start(f32[3,1024]{1,0:T(4,128)} %refs_1_.3) | copy-start | bytes 36868
  52.8 23.6 %copy-start.4 = (f32[8,136,128]{2,1,0:T(8,128)S(1)}, f32[8,136,128]{2,1,0:T(8,128)}, u32[]{:S(2)}) copy-start(f32[8,136,128]{2,1,0:T(8,128)} %copy-done.3) | copy-start | bytes 1671172
  58.3 28.1 %copy-start = (f32[8,64,256]{2,1,0:T(8,128)}, f32[8,64,256]{2,1,0:T(8,128)S(1)}, u32[]{:S(2)}) copy-start(f32[8,64,256]{2,1,0:T(8,128)S(1)} %all-to-all-done.2) | copy-start | bytes 1572868
  58.3 13.6 %all-to-all-start.4 = ((f32[8,64,256]{2,1,0:T(8,128)}), f32[8,64,256]{2,1,0:T(8,128)S(1)}, u32[]{:S(2)}, u32[]{:S(2)}) async-start(f32[8,64,256]{2,1,0:T(8,128)} %bitcast.7), calls=%async_computation.4 | async-start | bytes 1048576 | tf_op jit(solution)/shard_map/all_to_all | solution.py:368
  61.9 24.5 %collective-permute-start.3 = (f32[512,256]{1,0:T(8,128)S(1)}, f32[512,256]{1,0:T(8,128)S(1)}, u32[]{:S(2)}, u32[]{:S(2)}) collective-permute-start(f32[512,256]{1,0:T(8,128)S(1)} %bitcast.19), channel_id=1, source_target_pairs={{0,8},{8,0},{16,24},{24,16},{32,40},{40,32},{48,56},{56,48},{64,72... | collective-permute-start | bytes 1572872 | tf_op jit(solution)/shard_map/ppermute | solution.py:415
  72.8 13.6 %all-to-all-start.5 = ((f32[8,64,256]{2,1,0:T(8,128)}), f32[8,64,256]{2,1,0:T(8,128)S(1)}, u32[]{:S(2)}, u32[]{:S(2)}) async-start(f32[8,64,256]{2,1,0:T(8,128)} %broadcast_in_dim.11), calls=%async_computation.5 | async-start | bytes 1048576 | tf_op jit(solution)/shard_map/all_to_all | solution.py:368
  86.4 17.1 %copy-start.2 = (f32[8,64,256]{2,1,0:T(8,128)}, f32[8,64,256]{2,1,0:T(8,128)S(1)}, u32[]{:S(2)}) copy-start(f32[8,64,256]{2,1,0:T(8,128)S(1)} %all-to-all-done.5) | copy-start | bytes 1572868
  86.4 17.1 %collective-permute-start.5 = (f32[512,256]{1,0:T(8,128)S(1)}, f32[512,256]{1,0:T(8,128)S(1)}, u32[]{:S(2)}, u32[]{:S(2)}) collective-permute-start(f32[512,256]{1,0:T(8,128)S(1)} %bitcast.22), channel_id=1, source_target_pairs={{0,8},{8,0},{16,24},{24,16},{32,40},{40,32},{48,56},{56,48},{64,72... | collective-permute-start | bytes 1572872 | tf_op jit(solution)/shard_map/ppermute | solution.py:415
  86.4 0.8 copy-start.1
  93.8 17.3 %all-to-all-start.3 = ((f32[8,128,128]{2,1,0:T(8,128)}), f32[8,128,128]{2,1,0:T(8,128)S(1)}, u32[]{:S(2)}, u32[]{:S(2)}) async-start(f32[8,128,128]{2,1,0:T(8,128)} %give_back_feat.1), calls=%async_computation.3 | async-start | bytes 1048576 | tf_op jit(solution)/shard_map/all_to_all | solution.py:419
  100.9 15.0 %collective-permute-start.1 = (f32[272,256]{1,0:T(8,128)S(1)}, f32[272,256]{1,0:T(8,128)S(1)}, u32[]{:S(2)}, u32[]{:S(2)}) collective-permute-start(f32[272,256]{1,0:T(8,128)S(1)} %get-tuple-element.25), channel_id=1, source_target_pairs={{8,0},{16,8},{24,16},{32,24},{40,32},{48,40},{56,48},{64,56},{72,6... | collective-permute-start | bytes 835592 | tf_op jit(solution)/shard_map/ppermute | solution.py:407
  103.5 12.4 %collective-permute-start = (f32[272,256]{1,0:T(8,128)S(1)}, f32[272,256]{1,0:T(8,128)S(1)}, u32[]{:S(2)}, u32[]{:S(2)}) collective-permute-start(f32[272,256]{1,0:T(8,128)S(1)} %get-tuple-element.26), channel_id=1, source_target_pairs={{0,8},{8,16},{16,24},{24,32},{32,40},{40,48},{48,56},{56,64},{64,7... | collective-permute-start | bytes 835592 | tf_op jit(solution)/shard_map/ppermute | solution.py:406
  103.5 0.8 copy-start.5
  111.1 14.4 %all-to-all-start.6 = ((f32[8,128,128]{2,1,0:T(8,128)}), f32[8,128,128]{2,1,0:T(8,128)S(1)}, u32[]{:S(2)}, u32[]{:S(2)}) async-start(f32[8,128,128]{2,1,0:T(8,128)} %get-tuple-element.17), calls=%async_computation.6 | async-start | bytes 1048576 | tf_op jit(solution)/shard_map/all_to_all | solution.py:424
  115.9 0.7 copy-start.10
  116.6 0.7 copy-start.11
where the time goes:
time: 128 us; the launch traced here: 127 us
  Pallas kernels  39.8 us (31%)
  starting transfers between devices  38.2 us (30%)
  waiting for transfers between devices  32.9 us (26%)
  local copies, waits for them, and re-layouts  7.54 us (6%)
  other arithmetic  7.17 us (6%)
  between operations  1.52 us (1%)
    all_to_all x4, waiting for transfers between devices, exchange(): return lax.all_to_all(x, 'atom', 0, 0, axis_index_groups=chips, tiled=True)  28.8 us
    all_to_all x4, starting transfers between devices, exchange(): return lax.all_to_all(x, 'atom', 0, 0, axis_index_groups=chips, tiled=True)  17.2 us
    pallas_call x2, Pallas kernels, give_back_call(): pl.pallas_call(body, out_shape=tuple(out_shape), in_specs=[spec()] * len(...  13.4 us
    pallas_call x2, Pallas kernels, tables_call(): pl.pallas_call(body, out_shape=(jax.ShapeDtypeStruct((HALF, 2 * C), F32),...  12.9 us
    pallas_call x2, Pallas kernels, cot_call(): pl.pallas_call(cot_kernel, out_shape=jax.ShapeDtypeStruct((HALF, 2 * C),...  8.92 us
    all_to_all x1, starting transfers between devices, per_device(): long_parts = lax.all_to_all(long_part, 'mode', 0, 0, tiled=True)  6.97 us
    all_to_all x1, starting transfers between devices, per_device(): lax.all_to_all(jnp.broadcast_to(packed[None], (MODE_DEV, *packed.shape)),...  6.35 us
    all_to_all x1, starting transfers between devices, per_device(): back_parts = lax.all_to_all(back_part, 'mode', 0, 0, tiled=True)  4.82 us
  transfers between devices with their start and end apart: 13, of which 6 were waited for; matrix products, arithmetic and copies ran while one was open for 7% of the time, Pallas kernels for 26%

commit v1 on v0

v1 whole, which is shorter than its diff:
```python
import jax
import jax.numpy as jnp
from jax import lax
from jax.experimental import pallas as pl
from jax.experimental.pallas import tpu as pltpu
from jax.sharding import PartitionSpec as P

BLOCK = 128
REACH = 2
SLOTS = 5
C = 128
ATOMS = 1024
MODES = 1024
HALF = 512
SHARE = 64
RADIAL = 4
ATOM_DEV = 16
MODE_DEV = 8
HALO_ROWS = 272

F32 = jnp.float32
BF16 = jnp.bfloat16
MAGIC = 12582912.0
LIMIT = 24 * 1024 * 1024
VMEM = pltpu.VMEM

NT = (((1,), (1,)), ((), ()))
NN = (((1,), (0,)), ((), ()))


def dot(a, b, dims):
    return lax.dot_general(a, b, dims, preferred_element_type=F32)


def pieces(x):
    high = x.astype(BF16)
    low = (x - high.astype(F32)).astype(BF16)
    return high, low


def cos_sin_turns(t):
    r = t - ((t + MAGIC) - MAGIC)
    y = r * r
    s = r * (4.44287957 + y * (-7.30781668 + y * (3.59777418 + y * -0.79119939)))
    c = 1.4142135 + y * (
        -6.97885095 + y * (5.73946038 + y * (-1.88355791 + y * 0.31068803))
    )
    return 1.0 - s * s, s * c


ROWS = 32
TILE = 256
CHUNK = 4 * TILE
TILES = HALF // TILE


def columns_of(rows):
    rows = list(rows)
    rows = rows + [rows[0]] * (8 - len(rows))
    eight = jnp.concatenate(rows, axis=0)
    return jnp.concatenate([eight] * (BLOCK // 8), axis=0).T


def tables_tile(pos_ref, wave_ref, tab_ref, first, tile):
    shard = lax.axis_index("atom")
    mid = (2 * shard + 1).astype(F32) * (1.0 / 32.0)
    for group in range(TILE // BLOCK):
        at = tile * TILE + group * BLOCK
        w = wave_ref[:, pl.ds(pl.multiple_of(first + at, BLOCK), BLOCK)]
        start = ((w[0:1] * (2 * shard + 1)) & 31).astype(F32) * (1.0 / 32.0)
        wf = w.astype(F32)
        columns = columns_of((wf[0:1], wf[1:2], wf[2:3], start))
        for chunk in range(BLOCK // ROWS):
            part = columns[chunk * ROWS : (chunk + 1) * ROWS]
            w0, w1, w2, c0 = (
                jnp.broadcast_to(part[:, d : d + 1], (ROWS, BLOCK)) for d in range(4)
            )
            row = tile * CHUNK + group * BLOCK + chunk * ROWS
            for k in range(ATOMS // BLOCK):
                lanes = pl.ds(k * BLOCK, BLOCK)
                p0 = pos_ref[0:1, lanes] - mid
                p1 = pos_ref[1:2, lanes]
                p2 = pos_ref[2:3, lanes]
                t = w0 * p0 + (w1 * p1 + (w2 * p2 + c0))
                cos, sin = cos_sin_turns(t)
                ch, cl = pieces(cos)
                sh, sl = pieces(sin)
                tab_ref[row : row + ROWS, lanes] = ch
                tab_ref[TILE + row : TILE + row + ROWS, lanes] = sh
                tab_ref[2 * TILE + row : 2 * TILE + row + ROWS, lanes] = cl
                tab_ref[3 * TILE + row : 3 * TILE + row + ROWS, lanes] = sl


def sums_tile(tab_ref, rhs_ref, out_ref, tile, wide):
    at = tile * CHUNK
    both = dot(tab_ref[at : at + 2 * TILE, :], rhs_ref[...], NT)
    rest = dot(tab_ref[at + 2 * TILE : at + CHUNK, :], rhs_ref[0:wide, :], NT)
    total = both[:, :wide] + both[:, wide:] + rest
    for trig in range(2):
        out_ref[tile * TILE : (tile + 1) * TILE, trig * wide : (trig + 1) * wide] = (
            total[trig * TILE : (trig + 1) * TILE]
        )


def cot_rows(cot_ref, rhs_ref, high_at, low_at):
    for k in range(MODE_DEV):
        high, low = pieces(cot_ref[k, 0:C, :])
        rhs_ref[high_at : high_at + C, k * BLOCK : (k + 1) * BLOCK] = high
        rhs_ref[low_at : low_at + C, k * BLOCK : (k + 1) * BLOCK] = low


def tables_kernel(own, feat_hbm, pos_hbm, wave_hbm, extra_ref, *rest):
    out_ref, tab_hbm, rhs_ref, tab_ref, feat_ref, pos_ref, wave_ref, sems = rest
    fetches = [
        pltpu.make_async_copy(src, dst, sems.at[TILES + k])
        for k, (src, dst) in enumerate(
            ((pos_hbm, pos_ref), (wave_hbm, wave_ref), (feat_hbm, feat_ref))
        )
    ]
    for fetch in fetches:
        fetch.start()
    core = lax.axis_index("atom") % 2
    first = HALF * (core if own else 1 - core)
    wide = 2 * C if own else C
    if own:
        cot_rows(extra_ref, rhs_ref, C, wide + C)
    fetches[0].wait()
    fetches[1].wait()
    copies = []
    for tile in range(TILES):
        tables_tile(pos_ref, wave_ref, tab_ref, first, tile)
        rows = pl.ds(tile * CHUNK, CHUNK)
        copies.append(
            pltpu.make_async_copy(tab_ref.at[rows], tab_hbm.at[rows], sems.at[tile])
        )
        copies[-1].start()
        if tile == 0:
            fetches[2].wait()
            high, low = pieces(feat_ref[...])
            rhs_ref[0:C, :] = high
            rhs_ref[wide : wide + C, :] = low
        sums_tile(tab_ref, rhs_ref, out_ref, tile, wide)
    for copy in copies:
        copy.wait()


def spec():
    return pl.BlockSpec(memory_space=VMEM)


def call(body, name, ins, outs, scratch=(), flops=10**8, smem=(), far=(), far_outs=(), plain=(), args_in=()):
    args, in_specs = [], []
    for k, x in enumerate(ins):
        if k in smem:
            in_specs.append(pl.BlockSpec(memory_space=pltpu.SMEM))
        elif k in far:
            in_specs.append(pl.BlockSpec(memory_space=pltpu.HBM))
            x = pltpu.with_memory_space_constraint(x, pltpu.HBM)
        else:
            in_specs.append(spec())
            if k not in args_in:
                x = pltpu.with_memory_space_constraint(x, VMEM)
        args.append(x)
    size = sum(x.size * x.dtype.itemsize for x in ins)
    return pl.pallas_call(
        body,
        out_shape=tuple(
            pltpu.HBM(shape, kind)
            if k in far_outs
            else (jax.ShapeDtypeStruct if k in plain else VMEM)(shape, kind)
            for k, (shape, kind) in enumerate(outs)
        ),
        in_specs=in_specs,
        out_specs=tuple(
            pl.BlockSpec(memory_space=pltpu.HBM) if k in far_outs else spec()
            for k in range(len(outs))
        ),
        scratch_shapes=list(scratch),
        compiler_params=pltpu.CompilerParams(vmem_limit_bytes=LIMIT),
        cost_estimate=pl.CostEstimate(
            flops=flops, bytes_accessed=size, transcendentals=0
        ),
        name=name,
    )(*args)


def tables_call(own, feat, pos, wave, extra):
    def body(*refs):
        tables_kernel(own, *refs)

    wide = 2 * C if own else C
    return call(
        body,
        "tables_own" if own else "tables_other",
        (feat, pos, wave, extra),
        (((HALF, 2 * wide), F32), ((4 * HALF, ATOMS), BF16)),
        [
            VMEM((2 * wide, ATOMS), BF16),
            VMEM((4 * HALF, ATOMS), BF16),
            VMEM((C, ATOMS), F32),
            VMEM((3, ATOMS), F32),
            VMEM((3, MODES), jnp.int32),
            pltpu.SemaphoreType.DMA((TILES + 3,)),
        ],
        4 * 10**9,
        far=(0, 1, 2) if own else (0, 1, 2, 3),
        far_outs=(1,),
    )


def fetched(tab_hbm, tab_ref, sems):
    copies = []
    for tile in range(TILES):
        rows = pl.ds(tile * CHUNK, CHUNK)
        copy = pltpu.make_async_copy(tab_hbm.at[rows], tab_ref.at[rows], sems.at[tile])
        copy.start()
        copies.append(copy)
    return copies


def cot_kernel(cot_ref, tab_hbm, out_ref, rhs_ref, tab_ref, sems):
    copies = fetched(tab_hbm, tab_ref, sems)
    cot_rows(cot_ref, rhs_ref, 0, C)
    for tile in range(TILES):
        copies[tile].wait()
        sums_tile(tab_ref, rhs_ref, out_ref, tile, C)


def cot_call(cot, tab):
    (out,) = call(
        cot_kernel,
        "cot_sums",
        (cot, tab),
        (((HALF, 2 * C), F32),),
        [
            VMEM((2 * C, ATOMS), BF16),
            VMEM((4 * HALF, ATOMS), BF16),
            pltpu.SemaphoreType.DMA((TILES,)),
        ],
        2 * 10**9,
        far=(1,),
    )
    return out


def merge_kernel(own_ref, feat_ref, cot_ref, out_ref):
    for k in range(8):
        rows = slice(k * SHARE, (k + 1) * SHARE)
        for trig in range(2):
            for part in range(2):
                lanes = slice((2 * trig + part) * C, (2 * trig + part + 1) * C)
                got = (feat_ref, cot_ref)[part]
                out_ref[k, :, lanes] = (
                    own_ref[rows, lanes] + got[rows, trig * C : (trig + 1) * C]
                )


def give_back_kernel(own, sums_ref, filt_ref, tab_hbm, *rest):
    if own:
        acc_ref, lhs_ref, tab_ref, sems = rest
    else:
        acc_ref, out_ref, lhs_ref, tab_ref, sems = rest
    copies = fetched(tab_hbm, tab_ref, sems)
    core = lax.axis_index("atom") % 2
    at = pl.multiple_of(HALF * (core if own else 1 - core), HALF)
    scale = 1.0 / (ATOM_DEV * ATOMS)
    for k in range(HALF // C):
        filt = filt_ref[:, pl.ds(pl.multiple_of(at + k * C, C), C)] * scale
        tile, part = divmod(k * C, TILE)
        for trig in range(2):
            lanes = pl.ds((tile * 2 + trig) * TILE + part, C)
            for row in range(2):
                sums = sums_ref[k * C : (k + 1) * C, pl.ds((2 * trig + row) * C, C)]
                high, low = pieces(filt * sums.T)
                lhs_ref[row * C : (row + 1) * C, lanes] = high
                lhs_ref[(2 + row) * C : (3 + row) * C, lanes] = low
    width = 2 * BLOCK
    for n in range(TILES):
        copies[n].wait()
        depth = slice(n * 2 * TILE, (n + 1) * 2 * TILE)
        for k in range(ATOMS // width):
            lanes = slice(k * width, (k + 1) * width)
            top = n * CHUNK
            both = dot(lhs_ref[:, depth], tab_ref[top : top + 2 * TILE, lanes], NN)
            more = dot(
                lhs_ref[0 : 2 * C, depth],
                tab_ref[top + 2 * TILE : top + CHUNK, lanes],
                NN,
            )
            part = both[: 2 * C] + both[2 * C :] + more
            if not own and n == 0:
                part = part + acc_ref[:, lanes]
            if own and n == 0:
                acc_ref[:, lanes] = part
            elif own:
                acc_ref[:, lanes] = acc_ref[:, lanes] + part
            else:
                for side in range(2):
                    half = part[:, side * BLOCK : (side + 1) * BLOCK]
                    if n:
                        half = half + out_ref[2 * k + side]
                    out_ref[2 * k + side] = half


def give_back_call(own, sums, filt, tab, acc=None):
    def body(*refs):
        give_back_kernel(own, *refs)

    args = (sums, filt, tab) if own else (sums, filt, tab, acc)
    shape = (2 * C, ATOMS) if own else (MODE_DEV, 2 * C, BLOCK)
    (out,) = call(
        body,
        "give_back_own" if own else "give_back_other",
        args,
        ((shape, F32),),
        [
            VMEM((4 * C, 2 * HALF), BF16),
            VMEM((4 * HALF, ATOMS), BF16),
            pltpu.SemaphoreType.DMA((TILES,)),
        ],
        4 * 10**9,
        far=(2,),
        args_in=(1,),
    )
    return out


def grad_kernel(own_ref, oth_ref, grad_ref):
    core = lax.axis_index("atom") % 2
    scale = 1.0 / (ATOM_DEV * ATOMS)
    for half in range(2):
        ref = (own_ref, oth_ref)[half]
        at = pl.multiple_of(HALF * (core if half == 0 else 1 - core), HALF)
        for k in range(HALF // C):
            rows = slice(k * C, (k + 1) * C)
            grad = (
                ref[rows, 0:C] * ref[rows, C : 2 * C]
                + ref[rows, 2 * C : 3 * C] * ref[rows, 3 * C :]
            )
            grad_ref[:, pl.ds(pl.multiple_of(at + k * C, C), C)] = grad.T * scale


def near_kernel(
    left_ref,
    right_ref,
    feat_ref,
    pos_ref,
    cot_ref,
    mix_ref,
    rate_ref,
    out_ref,
    back_ref,
    ext_ref,
    rhs_ref,
):
    own = lax.axis_index("mode")
    pad = REACH * BLOCK
    ext_ref[:, 0:pad] = left_ref[...]
    ext_ref[:, pad + ATOMS :] = right_ref[...]
    ext_ref[0:C, pad : pad + ATOMS] = feat_ref[...]
    ext_ref[C : C + 3, pad : pad + ATOMS] = pos_ref[...]
    for k in range(MODE_DEV):
        ext_ref[136:272, pad + k * BLOCK : pad + (k + 1) * BLOCK] = cot_ref[k]
    shard = lax.axis_index("atom")
    total_blocks = ATOM_DEV * MODE_DEV

    def unit(block, row):
        return row * float(total_blocks) - block.astype(F32)

    def halves(row):
        q = row - 0.5
        y = q * q
        s = q * (
            3.14159265
            + y
            * (-5.16771276 + y * (2.55016332 + y * (-0.5992522 + y * (0.0820504 - 0.00702839 * y))))
        )
        c = 1.0 + y * (
            -4.93480214
            + y * (4.05870916 + y * (-1.335212 + y * (0.23493731 - 0.02439632 * y)))
        )
        return -s, c

    me = shard * MODE_DEV + own
    here = ext_ref[C : C + 8, pl.ds(pl.multiple_of(pad + own * BLOCK, BLOCK), BLOCK)]
    u_own = unit(me, here[0:1])
    c1, s1 = halves(here[1:2])
    c2, s2 = halves(here[2:3])
    columns = columns_of((u_own, c1, s1, c2, s2))
    wide = [jnp.broadcast_to(columns[:, k : k + 1], (BLOCK, BLOCK)) for k in range(5)]
    span = 2 * REACH + 1
    dist = []
    live = ext_ref[264:265, pl.ds(pl.multiple_of(pad + own * BLOCK, BLOCK), BLOCK)]
    for o in range(span):
        at = pl.ds(pl.multiple_of((own + o) * BLOCK, BLOCK), BLOCK)
        block = ext_ref[:, at]
        there = lax.rem(me + o - REACH + total_blocks, total_blocks)
        near = block[C : C + 8]
        x = wide[0] - (unit(there, near[0:1]) + float(o - REACH))
        d1c, d1s = halves(near[1:2])
        d2c, d2s = halves(near[2:3])
        y = x * x
        z = y * (3.14159265 / total_blocks) ** 2
        d = y * (1.0 + z * (-1.0 / 3.0 + z * (2.0 / 45.0)))
        e1 = wide[2] * d1c - wide[1] * d1s
        e2 = wide[4] * d2c - wide[3] * d2s
        d = d + (e1 * e1 + e2 * e2) * (2.0 / 3.14159265) ** 2
        dist.append(d)
        lanes = slice(o * BLOCK, (o + 1) * BLOCK)
        high, low = pieces(block[0:C] * live[0:1, o : o + 1])
        rhs_ref[0:C, lanes] = high
        rhs_ref[2 * C : 3 * C, lanes] = low
        lists_me = block[264:265, span - 1 - o : span - o]
        high, low = pieces(block[136 : 136 + C] * lists_me)
        rhs_ref[C : 2 * C, lanes] = high
        rhs_ref[3 * C :, lanes] = low
    out = ext_ref[0:C, pl.ds(pl.multiple_of(pad + own * BLOCK, BLOCK), BLOCK)]
    back = ext_ref[136 : 136 + C, pl.ds(pl.multiple_of(pad + own * BLOCK, BLOCK), BLOCK)]
    for r in range(RADIAL):
        rate = rate_ref[r]
        highs, lows = [], []
        for o in range(span):
            high, low = pieces(jnp.exp(dist[o] * -rate))
            highs.append(high)
            lows.append(low)
        weights_high = jnp.concatenate(highs, axis=1)
        weights_low = jnp.concatenate(lows, axis=1)
        both = dot(rhs_ref[...], weights_high, NT)
        got = (
            both[: 2 * C]
            + both[2 * C :]
            + dot(rhs_ref[0 : 2 * C, :], weights_low, NT)
        )
        high, low = pieces(got)
        mix = mix_ref[r]
        mh, ml = pieces(mix)
        th, tl = pieces(mix.T)
        out = out + (
            dot(th, high[:C], NN) + dot(th, low[:C], NN) + dot(tl, high[:C], NN)
        )
        back = back + (
            dot(mh, high[C:], NN) + dot(mh, low[C:], NN) + dot(ml, high[C:], NN)
        )
    out_ref[...] = out
    back_ref[...] = back


def near_call(left, right, feat, pos, cot, mix, rates):
    return call(
        near_kernel,
        "near_blocks",
        (left, right, feat, pos, cot, mix, rates),
        (((C, BLOCK), F32), ((C, BLOCK), F32)),
        [
            VMEM((HALO_ROWS, ATOMS + 2 * REACH * BLOCK), F32),
            VMEM((4 * C, (2 * REACH + 1) * BLOCK), BF16),
        ],
        2 * 10**9,
        smem=(6,),
        args_in=(2, 3, 5),
    )


def pack_kernel(ids_ref, live_ref, cot_ref, out_ref):
    total_blocks = ATOM_DEV * MODE_DEV
    me = lax.axis_index("atom") * MODE_DEV + lax.axis_index("mode")
    lane = lax.broadcasted_iota(jnp.int32, (8, BLOCK), 1)
    live = jnp.zeros((8, BLOCK), F32)
    for slot in range(SLOTS):
        offset = lax.rem(ids_ref[0, slot] - me + REACH + total_blocks, total_blocks)
        offset = jnp.where(slot < live_ref[0], offset, BLOCK)
        live = jnp.where(lane == offset, 1.0, live)
    for k in range(MODE_DEV):
        out_ref[k, 0:C, :] = cot_ref[...]
        out_ref[k, C:, :] = live


def halo_kernel(feat_hbm, pos_hbm, cot_ref, tail_ref, head_ref, pos_ref, sems):
    pad = REACH * BLOCK
    copies = []
    for k, (ref, first) in enumerate(((tail_ref, ATOMS - pad), (head_ref, 0))):
        lanes = pl.ds(first, pad)
        copies.append(
            pltpu.make_async_copy(
                feat_hbm.at[:, lanes], ref.at[pl.ds(0, C)], sems.at[k]
            )
        )
    copies.append(pltpu.make_async_copy(pos_hbm, pos_ref, sems.at[2]))
    for copy in copies:
        copy.start()
    for copy in copies:
        copy.wait()
    for ref, first in ((tail_ref, ATOMS - pad), (head_ref, 0)):
        ref[C : C + 8, :] = jnp.zeros((8, pad), F32)
        ref[C : C + 3, :] = pos_ref[:, first : first + pad]
        for k in range(REACH):
            lanes = slice(k * BLOCK, (k + 1) * BLOCK)
            ref[C + 8 :, lanes] = cot_ref[first // BLOCK + k]


def share_kernel(parts_ref, out_ref):
    share = parts_ref[0]
    for k in range(1, ATOM_DEV // 2):
        share = share + parts_ref[k]
    for k in range(ATOM_DEV // 2):
        out_ref[k] = share


def finish_kernel(near_ref, back_ref, parts_ref, out_ref, grad_ref):
    out = near_ref[...]
    grad = back_ref[...]
    for k in range(MODE_DEV):
        out = out + parts_ref[k, 0:C]
        grad = grad + parts_ref[k, C:]
    out_ref[...] = out
    grad_ref[...] = grad


def per_device(
    features,
    positions,
    wavevectors,
    mode_filter,
    radial_mix,
    radial_rates,
    neighbour_ids,
    live_counts,
    cotangent,
):
    core_swap = [(i, i ^ 1) for i in range(ATOM_DEV)]
    chips = [[c + 2 * i for i in range(ATOM_DEV // 2)] for c in range(2)]
    up = [(i, (i + 1) % ATOM_DEV) for i in range(ATOM_DEV)]
    down = [((i + 1) % ATOM_DEV, i) for i in range(ATOM_DEV)]

    def exchange(x):
        return lax.all_to_all(x, "atom", 0, 0, axis_index_groups=chips, tiled=True)

    (packed,) = call(
        pack_kernel,
        "pack_cot",
        (neighbour_ids, live_counts, cotangent),
        (((MODE_DEV, C + 8, BLOCK), F32),),
        smem=(0, 1),
        args_in=(2,),
        plain=(0,),
    )
    cot = lax.all_to_all(packed, "mode", 0, 0, tiled=True)

    f_oth, tab_oth = tables_call(False, features, positions, wavevectors, packed)
    f_got = lax.ppermute(f_oth, "atom", core_swap)
    c_got = lax.ppermute(cot_call(cot, tab_oth), "atom", core_swap)
    sums, tab_own = tables_call(True, features, positions, wavevectors, cot)
    tail, head = call(
        halo_kernel,
        "halo",
        (features, positions, cot),
        (((HALO_ROWS, REACH * BLOCK), F32), ((HALO_ROWS, REACH * BLOCK), F32)),
        [VMEM((3, ATOMS), F32), pltpu.SemaphoreType.DMA((3,))],
        far=(0, 1),
    )
    left = lax.ppermute(tail, "atom", up)
    right = lax.ppermute(head, "atom", down)
    sums, left, right = lax.optimization_barrier((sums, left, right))
    (parts,) = call(
        merge_kernel, "merge", (sums, f_got, c_got), (((8, SHARE, 4 * C), F32),)
    )
    parts = exchange(parts)
    near_out, near_back = near_call(
        left, right, features, positions, cot, radial_mix, radial_rates
    )

    parts, near_out, near_back = lax.optimization_barrier((parts, near_out, near_back))
    (share,) = call(share_kernel, "share", (parts,), ((parts.shape, F32),))
    own = exchange(share).reshape(HALF, 4 * C)
    oth = lax.ppermute(own, "atom", core_swap)
    acc = give_back_call(True, own, mode_filter, tab_own)
    back = give_back_call(False, oth, mode_filter, tab_oth, acc)
    back = lax.all_to_all(back, "mode", 0, 0, tiled=True)
    (grad_filter,) = call(
        grad_kernel, "grad_filter", (own, oth), (((C, MODES), F32),), plain=(0,), args_in=(0, 1)
    )
    layer_out, grad_features = call(
        finish_kernel,
        "finish",
        (near_out, near_back, back),
        (((C, BLOCK), F32), ((C, BLOCK), F32)),
        plain=(0, 1),
        args_in=(0, 1),
    )
    return (layer_out, grad_features, grad_filter)


def solution(mesh):
    in_specs = (
        P(None, "atom"),
        P(None, "atom"),
        P(None, "mode"),
        P(None, "mode"),
        P(),
        P(),
        P(("atom", "mode"), None),
        P(("atom", "mode")),
        P(None, ("atom", "mode")),
    )
    out_specs = (P(None, ("atom", "mode")), P(None, ("atom", "mode")), P(None, "mode"))
    return jax.shard_map(
        per_device, mesh=mesh, in_specs=in_specs, out_specs=out_specs, check_vma=False
    )
```

time: 128 us -> 109 us (0.85)
  blocking collectives: 0 us -> 22.5 us
  starting transfers between devices: 38.2 us -> 19.5 us
  Pallas kernels: 39.8 us -> 29.9 us
  other arithmetic: 7.17 us -> 0 us
  local copies, waits for them, and re-layouts: 7.54 us -> 4.09 us
  waiting for transfers between devices: 32.9 us -> 30.2 us
    all_to_all x0 -> x1, blocking collectives: none -> 22.5 us  [exchange(): return lax.all_to_all(x, 'atom', 0, 0, axis_index_groups=chips, tiled=True)]
    all_to_all x4 -> x1, waiting for transfers between devices: 28.8 us -> 11.3 us  [exchange(): return lax.all_to_all(x, 'atom', 0, 0, axis_index_groups=chips, tiled=True)]
    all_to_all x3 -> x2, waiting for transfers between devices: 4.06 us -> 18.9 us  [the longest x1 14.7 us: per_device(): back = lax.all_to_all(back, 'mode', 0, 0, tiled=True)]
    all_to_all x4 -> x1, starting transfers between devices: 17.2 us -> 4.02 us  [exchange(): return lax.all_to_all(x, 'atom', 0, 0, axis_index_groups=chips, tiled=True)]
    pallas_call x7 -> x12, Pallas kernels: 39.8 us -> 29.9 us  [call(): pl.pallas_call(body, out_shape=tuple((pltpu.HBM(shape, kind) if k in far_...]
    all_to_all x3 -> x2, starting transfers between devices: 18.1 us -> 9.91 us  [the longest x1 6.35 us: per_device(): cot = lax.all_to_all(packed, 'mode', 0, 0, tiled=True)]
    add x4 -> x0, other arithmetic: 6.82 us -> none  [the longest x1 1.96 us: per_device(): c_parts = exchange((c_own + c_got).reshape(8, SHARE, 2 * C))]
    ppermute x5 -> x4, starting transfers between devices: 2.8 us -> 5.52 us  [the longest x1 4.87 us: per_device(): right = lax.ppermute(head, 'atom', down)]
  transfers between devices with their start and end apart: 13 -> 8, of which waited for: 6 -> 3; matrix products, arithmetic and copies ran while one was open for 7% -> 0% of each run, Pallas kernels for 26% -> 21%
where the time goes in v1:
time: 109 us; the launch traced here: 108 us
  waiting for transfers between devices  30.2 us (28%)
  Pallas kernels  29.9 us (27%)
  blocking collectives  22.5 us (21%)
  starting transfers between devices  19.5 us (18%)
  local copies, waits for them, and re-layouts  4.09 us (4%)
  between operations  1.46 us (1%)
    pallas_call x12, Pallas kernels, call(): pl.pallas_call(body, out_shape=tuple((pltpu.HBM(shape, kind) if k in far_...  29.9 us
    all_to_all x1, blocking collectives, exchange(): return lax.all_to_all(x, 'atom', 0, 0, axis_index_groups=chips, tiled=True)  22.5 us
    all_to_all x1, waiting for transfers between devices, per_device(): back = lax.all_to_all(back, 'mode', 0, 0, tiled=True)  14.7 us
    all_to_all x1, waiting for transfers between devices, exchange(): return lax.all_to_all(x, 'atom', 0, 0, axis_index_groups=chips, tiled=True)  11.3 us
    all_to_all x1, starting transfers between devices, per_device(): cot = lax.all_to_all(packed, 'mode', 0, 0, tiled=True)  6.35 us
    ppermute x1, starting transfers between devices, per_device(): right = lax.ppermute(head, 'atom', down)  4.87 us
    all_to_all x1, waiting for transfers between devices, per_device(): cot = lax.all_to_all(packed, 'mode', 0, 0, tiled=True)  4.26 us
    unnamed x16, local copies, waits for them, and re-layouts  4.09 us
  transfers between devices with their start and end apart: 8, of which 3 were waited for; matrix products, arithmetic and copies ran while one was open for 0% of the time, Pallas kernels for 21%

profile of v1, /device:TPU:0, one launch (start us, length us, event | category | flops | bytes accessed | tf_op | source)
XLA Modules:
  0.0 107.8 jit_solution(2311528371732337152)
XLA Ops:
  1.3 0.0 copy-start.2
  1.3 0.8 copy-done.2
  2.1 0.0 copy-start.4
  2.1 0.7 copy-done.4
  2.8 1.4 %pack_cot.1.refs_3_ = f32[8,136,128]{2,1,0:T(8,128)} custom-call(s32[1,5]{1,0:T(1,128)S(1)} %copy-done.4, s32[1]{0:T(128)S(6)} %copy.12.live_ref, f32[128,128]{1,0:T(8,128)S(1)} %copy-done.2), custom_call_target="tpu_custom_call" | custom-call | flops 100000000 | bytes 65560 | tf_op jit(solution)/shard_map/pack_cot/pallas_call | solution.py:165
  4.2 6.4 %all-to-all-start = ((f32[8,136,128]{2,1,0:T(8,128)}), f32[8,136,128]{2,1,0:T(8,128)S(1)}, u32[]{:S(2)}, u32[]{:S(2)}) async-start(f32[8,136,128]{2,1,0:T(8,128)} %pack_cot.1.refs_3_), calls=%async_computation | async-start | bytes 1114112 | tf_op jit(solution)/shard_map/all_to_all | solution.py:547
  10.5 5.4 %tables_other.1 = (f32[512,256]{1,0:T(8,128)S(1)}, bf16[2048,1024]{1,0:T(8,128)(2,1)}) custom-call(f32[128,1024]{1,0:T(8,128)} %feat_ref.1, f32[3,1024]{1,0:T(4,128)} %pos_ref.1, s32[3,1024]{1,0:T(4,128)} %refs_2_.3, f32[8,136,128]{2,1,0:T(8,128)} %pack_cot.1.refs_3_), custom_call_target="tpu_custom_call" | custom-call | flops 4000000000 | bytes 1105920 | tf_op jit(solution)/shard_map/tables_other/pallas_call | solution.py:165
  15.9 0.1 collective-permute-start.2
  16.0 4.3 %all-to-all-done.refs_3_.cot_ref = f32[8,136,128]{2,1,0:T(8,128)S(1)} async-done(((f32[8,136,128]{2,1,0:T(8,128)}), f32[8,136,128]{2,1,0:T(8,128)S(1)}, u32[]{:S(2)}, u32[]{:S(2)}) %all-to-all-start) | async-done | bytes 557088 | tf_op jit(solution)/shard_map/all_to_all | solution.py:547
  20.3 3.1 %cot_sums.1 = f32[512,256]{1,0:T(8,128)S(1)} custom-call(f32[8,136,128]{2,1,0:T(8,128)S(1)} %all-to-all-done.refs_3_.cot_ref, bf16[2048,1024]{1,0:T(8,128)(2,1)} %get-tuple-element.24.tab_hbm.refs_2_), custom_call_target="tpu_custom_call" | custom-call | flops 2000000000 | bytes 4751360 | tf_op jit(solution)/shard_map/cot_sums/pallas_call | solution.py:165
  23.4 0.1 collective-permute-start.3
  23.5 1.0 halo.1
  24.5 0.6 collective-permute-start
  25.1 4.9 %collective-permute-start.1 = (f32[272,256]{1,0:T(8,128)S(1)}, f32[272,256]{1,0:T(8,128)S(1)}, u32[]{:S(2)}, u32[]{:S(2)}) collective-permute-start(f32[272,256]{1,0:T(8,128)S(1)} %get-tuple-element.21), channel_id=1, source_target_pairs={{8,0},{16,8},{24,16},{32,24},{40,32},{48,40},{56,48},{64,56},{72,6... | collective-permute-start | bytes 835592 | tf_op jit(solution)/shard_map/ppermute | solution.py:562
  29.9 5.4 %tables_own.1 = (f32[512,512]{1,0:T(8,128)S(1)}, bf16[2048,1024]{1,0:T(8,128)(2,1)}) custom-call(f32[128,1024]{1,0:T(8,128)} %feat_ref.1, f32[3,1024]{1,0:T(4,128)} %pos_ref.1, s32[3,1024]{1,0:T(4,128)} %refs_2_.3, f32[8,136,128]{2,1,0:T(8,128)S(1)} %all-to-all-done.refs_3_.cot_ref), custom_call_target="tpu_custom_call" | custom-call | flops 4000000000 | bytes 1105920 | tf_op jit(solution)/shard_map/tables_own/pallas_call | solution.py:165
  35.4 0.0 copy-start.1
  35.4 0.0 copy-start.3
  35.4 0.0 collective-permute-done.left_ref
  35.4 0.0 collective-permute-done.1.right_ref
  35.4 0.0 collective-permute-done.2.feat_ref
  35.4 0.0 collective-permute-done.3.cot_ref
  35.4 1.2 %merge.1 = f32[8,64,512]{2,1,0:T(8,128)} custom-call(f32[512,512]{1,0:T(8,128)S(1)} %get-tuple-element.22.own_ref, f32[512,256]{1,0:T(8,128)S(1)} %collective-permute-done.2.feat_ref, f32[512,256]{1,0:T(8,128)S(1)} %collective-permute-done.3.cot_ref), custom_call_target="tpu_custom_call" | custom-call | flops 100000000 | bytes 2097152 | tf_op jit(solution)/shard_map/merge/pallas_call | solution.py:165
  36.6 4.0 %all-to-all-start.1 = ((f32[8,64,512]{2,1,0:T(8,128)}), f32[8,64,512]{2,1,0:T(8,128)S(1)}, u32[]{:S(2)}, u32[]{:S(2)}) async-start(f32[8,64,512]{2,1,0:T(8,128)} %merge.1), calls=%async_computation.1 | async-start | bytes 2097152 | tf_op jit(solution)/shard_map/all_to_all | solution.py:536
  40.6 0.0 copy-done.1
  40.6 0.0 copy-done.3
  40.6 0.0 copy-start.6
  40.7 0.9 copy-done.6
  41.6 0.0 copy-start.7
  41.6 0.7 copy-done.7
  42.2 0.0 copy-start.5
  42.3 3.1 %near_blocks.1 = (f32[128,128]{1,0:T(8,128)S(1)}, f32[128,128]{1,0:T(8,128)S(1)}) custom-call(f32[272,256]{1,0:T(8,128)S(1)} %collective-permute-done.left_ref, f32[272,256]{1,0:T(8,128)S(1)} %collective-permute-done.1.right_ref, f32[128,1024]{1,0:T(8,128)S(1)} %copy-done.1, f32[3,1024]{1,0:T(4,128)S(1)} %copy-done.3, ...), custom_call_target="tpu_custom_call" | custom-call | flops 2000000000 | bytes 1912848 | tf_op jit(solution)/shard_map/near_blocks/pallas_call | solution.py:165
  45.3 11.3 %all-to-all-done.1.parts_ref = f32[8,64,512]{2,1,0:T(8,128)S(1)} async-done(((f32[8,64,512]{2,1,0:T(8,128)}), f32[8,64,512]{2,1,0:T(8,128)S(1)}, u32[]{:S(2)}, u32[]{:S(2)}) %all-to-all-start.1) | async-done | bytes 1048608 | tf_op jit(solution)/shard_map/all_to_all | solution.py:536
  56.6 0.1 share.1
  56.7 22.5 %all_to_all.20 = f32[8,64,512]{2,1,0:T(8,128)S(1)} all-to-all(f32[8,64,512]{2,1,0:T(8,128)S(1)} %share.1), channel_id=1, replica_groups={{0,16,32,48,64,80,96,112},{8,24,40,56,72,88,104,120},{1,17,33,49,65,81,..., dimensions={0} | all-to-all | bytes 2097152 | tf_op jit(solution)/shard_map/all_to_all | solution.py:536
  79.2 0.0 collective-permute-start.4
  79.2 0.0 copy-done.5
  79.2 3.8 %give_back_own.1.refs_3_ = f32[256,1024]{1,0:T(8,128)S(1)} custom-call(f32[512,512]{1,0:T(8,128)S(1)} %bitcast.2, f32[128,1024]{1,0:T(8,128)S(1)} %copy-done.5, bf16[2048,1024]{1,0:T(8,128)(2,1)} %get-tuple-element.32.refs_2_), custom_call_target="tpu_custom_call" | custom-call | flops 4000000000 | bytes 5767168 | tf_op jit(solution)/shard_map/give_back_own/pallas_call | solution.py:165
  83.0 0.0 collective-permute-done.4.refs_0_.oth_ref
  83.0 3.8 %give_back_other.1 = f32[8,256,128]{2,1,0:T(8,128)S(1)} custom-call(f32[512,512]{1,0:T(8,128)S(1)} %collective-permute-done.4.refs_0_.oth_ref, f32[128,1024]{1,0:T(8,128)S(1)} %copy-done.5, bf16[2048,1024]{1,0:T(8,128)(2,1)} %get-tuple-element.24.tab_hbm.refs_2_, f32[256,1024]{1,0:T(8,128)S(1)} %give_back_own.1.refs_3_), custom_call_target="tpu_custom_call" | custom-call | flops 4000000000 | bytes 6815744 | tf_op jit(solution)/shard_map/give_back_other/pallas_call | solution.py:165
  86.9 0.0 copy-start
  86.9 1.0 copy-done
  87.9 3.6 %all-to-all-start.3 = ((f32[8,256,128]{2,1,0:T(8,128)}), f32[8,256,128]{2,1,0:T(8,128)S(1)}, u32[]{:S(2)}, u32[]{:S(2)}) async-start(f32[8,256,128]{2,1,0:T(8,128)} %copy-done), calls=%async_computation.3 | async-start | bytes 2097152 | tf_op jit(solution)/shard_map/all_to_all | solution.py:578
  91.4 1.0 grad_filter.1
  92.4 14.7 %all-to-all-done.3.parts_ref = f32[8,256,128]{2,1,0:T(8,128)S(1)} async-done(((f32[8,256,128]{2,1,0:T(8,128)}), f32[8,256,128]{2,1,0:T(8,128)S(1)}, u32[]{:S(2)}, u32[]{:S(2)}) %all-to-all-start.3) | async-done | bytes 1048608 | tf_op jit(solution)/shard_map/all_to_all | solution.py:578
  107.1 0.7 finish.1
Async XLA Ops:
  1.3 0.8 copy-start.2
  2.1 0.7 copy-start.4
  4.2 16.1 %all-to-all-start = ((f32[8,136,128]{2,1,0:T(8,128)}), f32[8,136,128]{2,1,0:T(8,128)S(1)}, u32[]{:S(2)}, u32[]{:S(2)}) async-start(f32[8,136,128]{2,1,0:T(8,128)} %pack_cot.1.refs_3_), calls=%async_computation | async-start | bytes 1114112 | tf_op jit(solution)/shard_map/all_to_all | solution.py:547
  15.9 19.5 %collective-permute-start.2 = (f32[512,256]{1,0:T(8,128)S(1)}, f32[512,256]{1,0:T(8,128)S(1)}, u32[]{:S(2)}, u32[]{:S(2)}) collective-permute-start(f32[512,256]{1,0:T(8,128)S(1)} %get-tuple-element.23), channel_id=1, source_target_pairs={{0,8},{8,0},{16,24},{24,16},{32,40},{40,32},{48,56},{56,48},{64,72... | collective-permute-start | bytes 1572872 | tf_op jit(solution)/shard_map/ppermute | solution.py:550
  23.4 12.1 %collective-permute-start.3 = (f32[512,256]{1,0:T(8,128)S(1)}, f32[512,256]{1,0:T(8,128)S(1)}, u32[]{:S(2)}, u32[]{:S(2)}) collective-permute-start(f32[512,256]{1,0:T(8,128)S(1)} %cot_sums.1), channel_id=1, source_target_pairs={{0,8},{8,0},{16,24},{24,16},{32,40},{40,32},{48,56},{56,48},{64,72... | collective-permute-start | bytes 1572872 | tf_op jit(solution)/shard_map/ppermute | solution.py:551
  24.5 10.9 %collective-permute-start = (f32[272,256]{1,0:T(8,128)S(1)}, f32[272,256]{1,0:T(8,128)S(1)}, u32[]{:S(2)}, u32[]{:S(2)}) collective-permute-start(f32[272,256]{1,0:T(8,128)S(1)} %get-tuple-element.20), channel_id=1, source_target_pairs={{0,8},{8,16},{16,24},{24,32},{32,40},{40,48},{48,56},{56,64},{64,7... | collective-permute-start | bytes 835592 | tf_op jit(solution)/shard_map/ppermute | solution.py:561
  25.1 10.4 %collective-permute-start.1 = (f32[272,256]{1,0:T(8,128)S(1)}, f32[272,256]{1,0:T(8,128)S(1)}, u32[]{:S(2)}, u32[]{:S(2)}) collective-permute-start(f32[272,256]{1,0:T(8,128)S(1)} %get-tuple-element.21), channel_id=1, source_target_pairs={{8,0},{16,8},{24,16},{32,24},{40,32},{48,40},{56,48},{64,56},{72,6... | collective-permute-start | bytes 835592 | tf_op jit(solution)/shard_map/ppermute | solution.py:562
  35.4 5.2 %copy-start.1 = (f32[128,1024]{1,0:T(8,128)S(1)}, f32[128,1024]{1,0:T(8,128)}, u32[]{:S(2)}) copy-start(f32[128,1024]{1,0:T(8,128)} %feat_ref.1) | copy-start | bytes 1572868
  35.4 5.2 %copy-start.3 = (f32[3,1024]{1,0:T(4,128)S(1)}, f32[3,1024]{1,0:T(4,128)}, u32[]{:S(2)}) copy-start(f32[3,1024]{1,0:T(4,128)} %pos_ref.1) | copy-start | bytes 36868
  36.6 20.0 %all-to-all-start.1 = ((f32[8,64,512]{2,1,0:T(8,128)}), f32[8,64,512]{2,1,0:T(8,128)S(1)}, u32[]{:S(2)}, u32[]{:S(2)}) async-start(f32[8,64,512]{2,1,0:T(8,128)} %merge.1), calls=%async_computation.1 | async-start | bytes 2097152 | tf_op jit(solution)/shard_map/all_to_all | solution.py:536
  40.6 1.0 copy-start.6
  41.6 0.7 copy-start.7
  42.2 37.0 %copy-start.5 = (f32[128,1024]{1,0:T(8,128)S(1)}, f32[128,1024]{1,0:T(8,128)}, u32[]{:S(2)}) copy-start(f32[128,1024]{1,0:T(8,128)} %refs_1_.7) | copy-start | bytes 1572868
  79.2 3.8 %collective-permute-start.4 = (f32[512,512]{1,0:T(8,128)S(1)}, f32[512,512]{1,0:T(8,128)S(1)}, u32[]{:S(2)}, u32[]{:S(2)}) collective-permute-start(f32[512,512]{1,0:T(8,128)S(1)} %bitcast.1), channel_id=1, source_target_pairs={{0,8},{8,0},{16,24},{24,16},{32,40},{40,32},{48,56},{56,48},{64,72... | collective-permute-start | bytes 3145736 | tf_op jit(solution)/shard_map/ppermute | solution.py:575
  86.9 1.0 copy-start
  87.9 19.2 %all-to-all-start.3 = ((f32[8,256,128]{2,1,0:T(8,128)}), f32[8,256,128]{2,1,0:T(8,128)S(1)}, u32[]{:S(2)}, u32[]{:S(2)}) async-start(f32[8,256,128]{2,1,0:T(8,128)} %copy-done), calls=%async_computation.3 | async-start | bytes 2097152 | tf_op jit(solution)/shard_map/all_to_all | solution.py:578
